TPU v7x, 32 devices: a whole 2x2x4 slice. The times are simulated.
32 devices in a mesh: dp: 4 (over y, x), ctx: 8 (over z, core).
Axes of the slice: x: 2, y: 2, z: 4, core: 2. Of those that a mesh axis runs over, the one named last changes fastest.
Arguments:
- inputs: float32 [4, 1024, 1088], P('dp', 'ctx'), may hold values from -6 to 6
- out_grad: float32 [4, 1024, 1088], P('dp', 'ctx'), may hold values from -6 to 6
- pair_blocks: int32 [8, 2], replicated, may hold values from 0 to 15, as said below
- triple_weight: float32 [1088, 3264], P('ctx', 'dp')
- merge_weight: float32 [1088, 1088], P('ctx', 'dp'), may hold values from -0.75 to 0.75
- expand_weight: float32 [1088, 4352], P('ctx', 'dp'), may hold values from -0.1875 to 0.1875
- shrink_weight: float32 [4352, 1088], P('ctx', 'dp'), may hold values from -0.09375 to 0.09375
- vector_params: float32 [1088, 12], P('ctx', 'dp')
- triple_moment: float32 [1088, 3264], P('ctx', 'dp'), may hold values from -24 to 24
- merge_moment: float32 [1088, 1088], P('ctx', 'dp'), may hold values from -6 to 6
- expand_moment: float32 [1088, 4352], P('ctx', 'dp'), may hold values from -6 to 6
- shrink_moment: float32 [4352, 1088], P('ctx', 'dp'), may hold values from -6 to 6
- vector_moment: float32 [1088, 12], P('ctx', 'dp'), may hold values from -112 to 112
- triple_square: float32 [1088, 3264], P('ctx', 'dp'), may hold values from 24.576 to 245.76
- merge_square: float32 [1088, 1088], P('ctx', 'dp'), may hold values from 8.192 to 81.92
- expand_square: float32 [1088, 4352], P('ctx', 'dp'), may hold values from 8.192 to 81.92
- shrink_square: float32 [4352, 1088], P('ctx', 'dp'), may hold values from 8.192 to 81.92
- vector_square: float32 [1088, 12], P('ctx', 'dp'), may hold values from 204.8 to 2048
Outputs:
- block_output: float32 [4, 1024, 1088], P('dp', 'ctx')
- input_grad: float32 [4, 1024, 1088], P('dp', 'ctx')
- triple_grad: float32 [1088, 3264], P('ctx', 'dp')
- merge_grad: float32 [1088, 1088], P('ctx', 'dp')
- expand_grad: float32 [1088, 4352], P('ctx', 'dp')
- shrink_grad: float32 [4352, 1088], P('ctx', 'dp')
- vector_grad: float32 [1088, 12], P('ctx', 'dp')
- triple_new: float32 [1088, 3264], P('ctx', 'dp')
- merge_new: float32 [1088, 1088], P('ctx', 'dp')
- expand_new: float32 [1088, 4352], P('ctx', 'dp')
- shrink_new: float32 [4352, 1088], P('ctx', 'dp')
- vector_new: float32 [1088, 12], P('ctx', 'dp')
- triple_moment_new: float32 [1088, 3264], P('ctx', 'dp')
- merge_moment_new: float32 [1088, 1088], P('ctx', 'dp')
- expand_moment_new: float32 [1088, 4352], P('ctx', 'dp')
- shrink_moment_new: float32 [4352, 1088], P('ctx', 'dp')
- vector_moment_new: float32 [1088, 12], P('ctx', 'dp')
- triple_square_new: float32 [1088, 3264], P('ctx', 'dp')
- merge_square_new: float32 [1088, 1088], P('ctx', 'dp')
- expand_square_new: float32 [1088, 4352], P('ctx', 'dp')
- shrink_square_new: float32 [4352, 1088], P('ctx', 'dp')
- vector_square_new: float32 [1088, 12], P('ctx', 'dp')
Inputs may be any that keep to these rules, and one draw needn't show every extreme that they name: `pair_blocks`: row c names the two blocks of 64 positions that stand in stored rows c * 2 * 64 onward: first a block p, then 2 * 8 - 1 - p; each of the 16 blocks is named once.
All inputs are finite; a program needn't handle non-finite values.
Results may differ from a plain program's by a relative error of at most 0.011.
Values may be sent and summed in bfloat16 or wider, within the bound.
A program may use at most 256 MiB of HBM per device.

v0:
```python
import jax
import jax.numpy as jnp
from jax import lax
from jax.sharding import PartitionSpec as P

D = 1088
H = 17
HD = 64
BLK = 64
norm_eps = 1e-05
beta_first = 0.9
beta_second = 0.95
learn_rate = 0.01
decay_rate = 0.1
adam_eps = 1e-08
adam_steps = 4
gelu_coef = 0.7978845608028654
masked_score = -1e30


def layer_norm(values):
    center = jnp.mean(values, axis=-1, keepdims=True)
    shifted = values - center
    inverse = lax.rsqrt(jnp.mean(shifted * shifted, axis=-1, keepdims=True) + norm_eps)
    return (shifted * inverse, inverse)


def norm_back(incoming, normed, inverse, gain_vec):
    scaled = incoming * gain_vec
    return inverse * (
        scaled
        - jnp.mean(scaled, axis=-1, keepdims=True)
        - normed * jnp.mean(scaled * normed, axis=-1, keepdims=True)
    )


def gelu_value(values):
    inside = gelu_coef * (values + 0.044715 * values * values * values)
    return 0.5 * values * (1.0 + jnp.tanh(inside))


def gelu_slope(values):
    inside = gelu_coef * (values + 0.044715 * values * values * values)
    tangent = jnp.tanh(inside)
    return 0.5 * (1.0 + tangent) + 0.5 * values * (1.0 - tangent * tangent) * gelu_coef * (
        1.0 + 3.0 * 0.044715 * values * values
    )


def adam_update(weight, gradient, moment, square, decayed):
    moment_new = beta_first * moment + (1.0 - beta_first) * gradient
    square_new = beta_second * square + (1.0 - beta_second) * gradient * gradient
    first_fix = 1.0 - beta_first**adam_steps
    second_fix = 1.0 - beta_second**adam_steps
    direction = moment_new / first_fix / (jnp.sqrt(square_new / second_fix) + adam_eps)
    if decayed:
        direction = direction + decay_rate * weight
    return (weight - learn_rate * direction, moment_new, square_new)


def split_heads(values):
    return values.reshape(values.shape[0], H, HD).transpose(1, 0, 2)


def join_heads(values):
    return values.transpose(1, 0, 2).reshape(values.shape[1], H * HD)


def gather_params(first_part, second_part, third_part, fourth_part, fifth_part):
    piece_one, piece_two, piece_three, piece_four, piece_five = (
        lax.all_gather(first_part, "ctx", axis=0, tiled=True),
        lax.all_gather(second_part, "ctx", axis=0, tiled=True),
        lax.all_gather(third_part, "ctx", axis=0, tiled=True),
        lax.all_gather(fourth_part, "ctx", axis=0, tiled=True),
        lax.all_gather(fifth_part, "ctx", axis=0, tiled=True),
    )
    return (
        lax.all_gather(piece_one, "dp", axis=1, tiled=True),
        lax.all_gather(piece_two, "dp", axis=1, tiled=True),
        lax.all_gather(piece_three, "dp", axis=1, tiled=True),
        lax.all_gather(piece_four, "dp", axis=1, tiled=True),
        lax.all_gather(piece_five, "dp", axis=1, tiled=True),
    )


def reduce_grads(first_part, second_part, third_part, fourth_part, fifth_part):
    piece_one, piece_two, piece_three, piece_four, piece_five = (
        lax.psum_scatter(first_part, "ctx", scatter_dimension=0, tiled=True),
        lax.psum_scatter(second_part, "ctx", scatter_dimension=0, tiled=True),
        lax.psum_scatter(third_part, "ctx", scatter_dimension=0, tiled=True),
        lax.psum_scatter(fourth_part, "ctx", scatter_dimension=0, tiled=True),
        lax.psum_scatter(fifth_part, "ctx", scatter_dimension=0, tiled=True),
    )
    return (
        lax.psum_scatter(piece_one, "dp", scatter_dimension=1, tiled=True),
        lax.psum_scatter(piece_two, "dp", scatter_dimension=1, tiled=True),
        lax.psum_scatter(piece_three, "dp", scatter_dimension=1, tiled=True),
        lax.psum_scatter(piece_four, "dp", scatter_dimension=1, tiled=True),
        lax.psum_scatter(piece_five, "dp", scatter_dimension=1, tiled=True),
    )


def gather_keys(key_rows, value_rows):
    return (
        lax.all_gather(key_rows, "ctx", axis=0, tiled=True),
        lax.all_gather(value_rows, "ctx", axis=0, tiled=True),
    )


def local(
    inputs,
    out_grad,
    pair_blocks,
    triple_weight,
    merge_weight,
    expand_weight,
    shrink_weight,
    vector_params,
    triple_moment,
    merge_moment,
    expand_moment,
    shrink_moment,
    vector_moment,
    triple_square,
    merge_square,
    expand_square,
    shrink_square,
    vector_square,
):
    rows_here = inputs.shape[1]
    stream = inputs[0]
    cotangent = out_grad[0]
    offsets = jnp.arange(BLK, dtype=jnp.int32)
    all_positions = (pair_blocks.reshape(-1)[:, None] * BLK + offsets[None, :]).reshape(-1)
    query_positions = lax.dynamic_slice_in_dim(
        all_positions, lax.axis_index("ctx") * rows_here, rows_here
    )
    allowed = query_positions[:, None] >= all_positions[None, :]
    score_scale = HD ** (-0.5)
    copy_triple = triple_weight.astype(jnp.bfloat16)
    copy_merge = merge_weight.astype(jnp.bfloat16)
    copy_expand = expand_weight.astype(jnp.bfloat16)
    copy_shrink = shrink_weight.astype(jnp.bfloat16)
    copy_vector = vector_params.astype(jnp.bfloat16)
    w_triple, w_merge, w_expand, w_shrink, w_vector = gather_params(
        copy_triple, copy_merge, copy_expand, copy_shrink, copy_vector
    )
    vectors = w_vector.astype(jnp.float32)
    gain_one = vectors[:, 0]
    shift_one = vectors[:, 1]
    query_bias = vectors[:, 2]
    value_bias = vectors[:, 3]
    merge_bias = vectors[:, 4]
    gain_two = vectors[:, 5]
    shift_two = vectors[:, 6]
    shrink_bias = vectors[:, 7]
    expand_bias = vectors[:, 8:12].T.reshape(-1)
    normed_one, inverse_one = layer_norm(stream)
    act_one = (normed_one * gain_one + shift_one).astype(jnp.bfloat16)
    triple = jnp.dot(act_one, w_triple, preferred_element_type=jnp.float32)
    query_b = (triple[:, :D] + query_bias).astype(jnp.bfloat16)
    key_b = triple[:, D : 2 * D].astype(jnp.bfloat16)
    value_b = (triple[:, 2 * D :] + value_bias).astype(jnp.bfloat16)
    keys_all, values_all = gather_keys(key_b, value_b)

    def head_scores(query_h, key_h):
        scores = (
            lax.dot_general(
                query_h, key_h, (((1,), (1,)), ((), ())), preferred_element_type=jnp.float32
            )
            * score_scale
        )
        return jnp.where(allowed, scores, masked_score)

    def head_forward(operands):
        query_h, key_h, value_h = operands
        scores = head_scores(query_h, key_h)
        row_max = jnp.max(scores, axis=1, keepdims=True)
        log_total = row_max + jnp.log(jnp.sum(jnp.exp(scores - row_max), axis=1, keepdims=True))
        probs_b = jnp.exp(scores - log_total).astype(jnp.bfloat16)
        attended = jnp.dot(probs_b, value_h, preferred_element_type=jnp.float32)
        return (attended.astype(jnp.bfloat16), log_total[:, 0])

    heads_query = split_heads(query_b)
    heads_key = split_heads(keys_all)
    heads_value = split_heads(values_all)
    heads_out, heads_total = lax.map(head_forward, (heads_query, heads_key, heads_value))
    attended_b = join_heads(heads_out)
    middle = stream + jnp.dot(attended_b, w_merge, preferred_element_type=jnp.float32) + merge_bias
    normed_two, inverse_two = layer_norm(middle)
    act_two = (normed_two * gain_two + shift_two).astype(jnp.bfloat16)
    pre_act = jnp.dot(act_two, w_expand, preferred_element_type=jnp.float32) + expand_bias
    hidden_b = gelu_value(pre_act).astype(jnp.bfloat16)
    block_out = (
        middle + jnp.dot(hidden_b, w_shrink, preferred_element_type=jnp.float32) + shrink_bias
    )
    back_triple, back_merge, back_expand, back_shrink, unused_vector = gather_params(
        copy_triple, copy_merge, copy_expand, copy_shrink, copy_vector
    )
    keys_again, values_again = gather_keys(key_b, value_b)
    back_key = split_heads(keys_again)
    back_value = split_heads(values_again)
    cotangent_b = cotangent.astype(jnp.bfloat16)
    shrink_local = jnp.dot(hidden_b.T, cotangent_b, preferred_element_type=jnp.float32)
    shrink_bias_grad = jnp.sum(cotangent, axis=0)
    dpre = jnp.dot(cotangent_b, back_shrink.T, preferred_element_type=jnp.float32) * gelu_slope(
        pre_act
    )
    dpre_b = dpre.astype(jnp.bfloat16)
    expand_local = jnp.dot(act_two.T, dpre_b, preferred_element_type=jnp.float32)
    expand_bias_grad = jnp.sum(dpre, axis=0)
    dact_two = jnp.dot(dpre_b, back_expand.T, preferred_element_type=jnp.float32)
    gain_two_grad = jnp.sum(dact_two * normed_two, axis=0)
    shift_two_grad = jnp.sum(dact_two, axis=0)
    dmiddle = cotangent + norm_back(dact_two, normed_two, inverse_two, gain_two)
    dmiddle_b = dmiddle.astype(jnp.bfloat16)
    merge_local = jnp.dot(attended_b.T, dmiddle_b, preferred_element_type=jnp.float32)
    merge_bias_grad = jnp.sum(dmiddle, axis=0)
    dattended_b = jnp.dot(dmiddle_b, back_merge.T, preferred_element_type=jnp.float32).astype(
        jnp.bfloat16
    )

    def head_backward(operands):
        query_h, key_h, value_h, out_h, dout_h, log_total = operands
        scores = head_scores(query_h, key_h)
        probs = jnp.exp(scores - log_total[:, None])
        probs_b = probs.astype(jnp.bfloat16)
        delta = jnp.sum(
            dout_h.astype(jnp.float32) * out_h.astype(jnp.float32), axis=1, keepdims=True
        )
        dprobs = lax.dot_general(
            dout_h, value_h, (((1,), (1,)), ((), ())), preferred_element_type=jnp.float32
        )
        dscores_b = (probs * (dprobs - delta) * score_scale).astype(jnp.bfloat16)
        dquery_h = jnp.dot(dscores_b, key_h, preferred_element_type=jnp.float32)
        dkey_h = lax.dot_general(
            dscores_b, query_h, (((0,), (0,)), ((), ())), preferred_element_type=jnp.float32
        )
        dvalue_h = lax.dot_general(
            probs_b, dout_h, (((0,), (0,)), ((), ())), preferred_element_type=jnp.float32
        )
        return (dquery_h, dkey_h, dvalue_h)

    dquery_heads, dkey_heads, dvalue_heads = lax.map(
        head_backward,
        (heads_query, back_key, back_value, heads_out, split_heads(dattended_b), heads_total),
    )
    dquery = join_heads(dquery_heads)
    dkey_rows, dvalue_rows = (
        lax.psum_scatter(join_heads(dkey_heads), "ctx", scatter_dimension=0, tiled=True),
        lax.psum_scatter(join_heads(dvalue_heads), "ctx", scatter_dimension=0, tiled=True),
    )
    dtriple_b = jnp.concatenate([dquery, dkey_rows, dvalue_rows], axis=1).astype(jnp.bfloat16)
    triple_local = jnp.dot(act_one.T, dtriple_b, preferred_element_type=jnp.float32)
    query_bias_grad = jnp.sum(dquery, axis=0)
    value_bias_grad = jnp.sum(dvalue_rows, axis=0)
    dact_one = jnp.dot(dtriple_b, back_triple.T, preferred_element_type=jnp.float32)
    gain_one_grad = jnp.sum(dact_one * normed_one, axis=0)
    shift_one_grad = jnp.sum(dact_one, axis=0)
    input_rows = dmiddle + norm_back(dact_one, normed_one, inverse_one, gain_one)
    vector_local = jnp.concatenate(
        [
            jnp.stack(
                [
                    gain_one_grad,
                    shift_one_grad,
                    query_bias_grad,
                    value_bias_grad,
                    merge_bias_grad,
                    gain_two_grad,
                    shift_two_grad,
                    shrink_bias_grad,
                ],
                axis=1,
            ),
            expand_bias_grad.reshape(4, D).T,
        ],
        axis=1,
    )
    triple_grad, merge_grad, expand_grad, shrink_grad, vector_grad = reduce_grads(
        triple_local, merge_local, expand_local, shrink_local, vector_local
    )
    triple_new, triple_moment_new, triple_square_new = adam_update(
        triple_weight, triple_grad, triple_moment, triple_square, True
    )
    merge_new, merge_moment_new, merge_square_new = adam_update(
        merge_weight, merge_grad, merge_moment, merge_square, True
    )
    expand_new, expand_moment_new, expand_square_new = adam_update(
        expand_weight, expand_grad, expand_moment, expand_square, True
    )
    shrink_new, shrink_moment_new, shrink_square_new = adam_update(
        shrink_weight, shrink_grad, shrink_moment, shrink_square, True
    )
    vector_new, vector_moment_new, vector_square_new = adam_update(
        vector_params, vector_grad, vector_moment, vector_square, False
    )
    return (
        block_out[None],
        input_rows[None],
        triple_grad,
        merge_grad,
        expand_grad,
        shrink_grad,
        vector_grad,
        triple_new,
        merge_new,
        expand_new,
        shrink_new,
        vector_new,
        triple_moment_new,
        merge_moment_new,
        expand_moment_new,
        shrink_moment_new,
        vector_moment_new,
        triple_square_new,
        merge_square_new,
        expand_square_new,
        shrink_square_new,
        vector_square_new,
    )


def solution(mesh):
    in_specs = (
        P("dp", "ctx", None),
        P("dp", "ctx", None),
        P(),
        P("ctx", "dp"),
        P("ctx", "dp"),
        P("ctx", "dp"),
        P("ctx", "dp"),
        P("ctx", "dp"),
        P("ctx", "dp"),
        P("ctx", "dp"),
        P("ctx", "dp"),
        P("ctx", "dp"),
        P("ctx", "dp"),
        P("ctx", "dp"),
        P("ctx", "dp"),
        P("ctx", "dp"),
        P("ctx", "dp"),
        P("ctx", "dp"),
    )
    out_specs = (
        P("dp", "ctx", None),
        P("dp", "ctx", None),
        P("ctx", "dp"),
        P("ctx", "dp"),
        P("ctx", "dp"),
        P("ctx", "dp"),
        P("ctx", "dp"),
        P("ctx", "dp"),
        P("ctx", "dp"),
        P("ctx", "dp"),
        P("ctx", "dp"),
        P("ctx", "dp"),
        P("ctx", "dp"),
        P("ctx", "dp"),
        P("ctx", "dp"),
        P("ctx", "dp"),
        P("ctx", "dp"),
        P("ctx", "dp"),
        P("ctx", "dp"),
        P("ctx", "dp"),
        P("ctx", "dp"),
        P("ctx", "dp"),
    )
    return jax.shard_map(local, mesh=mesh, in_specs=in_specs, out_specs=out_specs, check_vma=False)
```

profile of v0, /device:TPU:0, one launch (start us, length us, event | category | flops | bytes accessed | tf_op | source)
XLA Modules:
  0.0 1586.2 jit_solution(11072138455714467575)
XLA Ops:
  9.1 31.8 %all-gather.13.cloned.1.call-done = bf16[1088,816]{1,0:T(8,128)(2,1)} async-done(((bf16[136,816]{1,0:T(8,128)(2,1)}), bf16[1088,816]{1,0:T(8,128)(2,1)}) %all-gather.13.cloned.1.call-update) | async-done | bytes 1775632 | tf_op jit(solution)/shard_map/all_gather | solution.py:71
  46.9 12.8 all-gather
  59.8 8.8 all-gather.1
  69.6 55.4 %all-gather.15.cloned.1.call-done = bf16[1088,3264]{0,1:T(8,128)(2,1)} async-done(((bf16[1088,816]{0,1:T(8,128)(2,1)}), bf16[1088,3264]{0,1:T(8,128)(2,1)}) %all-gather.15.cloned.1.call-update) | async-done | bytes 7102480 | tf_op jit(solution)/shard_map/all_gather | solution.py:78
  125.0 5.4 fusion.75
  132.6 21.3 %all_gather.52 = bf16[1088,272]{1,0:T(8,128)(2,1)S(1)} all-gather(bf16[136,272]{1,0:T(8,128)(2,1)S(1)} %convert_element_type.74), channel_id=1, replica_groups=mesh['dp'=4,'ctx'=8] {'ctx'}, dimensions={0}, use_global_device_ids=true | all-gather | bytes 665856 | tf_op jit(solution)/shard_map/all_gather | solution.py:72
  155.0 11.0 all-gather.23.cloned.1.call-done
  173.4 28.5 %all-gather.29.cloned.1.call-done = bf16[8,544,272]{1,2,0:T(8,128)(2,1)} async-done(((bf16[1,544,272]{1,2,0:T(8,128)(2,1)}), bf16[8,544,272]{1,2,0:T(8,128)(2,1)}) %all-gather.29.cloned.1.call-update) | async-done | bytes 2367504 | tf_op jit(solution)/shard_map/all_gather | solution.py:74
  208.6 26.0 %all-gather.17.cloned.1.call-done = bf16[1024,1088]{0,1:T(8,128)(2,1)} async-done(((bf16[128,1088]{0,1:T(8,128)(2,1)}), bf16[1024,1088]{0,1:T(8,128)(2,1)}) %all-gather.17.cloned.1.call-update) | async-done | bytes 2228240 | tf_op jit(solution)/shard_map/all_gather | solution.py:105
  239.9 27.4 %all-gather.19.cloned.1.call-done = bf16[1024,1088]{0,1:T(8,128)(2,1)} async-done(((bf16[128,1088]{0,1:T(8,128)(2,1)}), bf16[1024,1088]{0,1:T(8,128)(2,1)}) %all-gather.19.cloned.1.call-update) | async-done | bytes 2228240 | tf_op jit(solution)/shard_map/all_gather | solution.py:106
  272.6 69.9 %while.28 = (s32[]{:T(128)}, bf16[17,128,64]{1,2,0:T(8,128)(2,1)S(1)}, f32[17,128]{1,0:T(8,128)}, bf16[17,128,64]{2,1,0:T(8,128)(2,1)S(1)}, bf16[17,1024,64]{2,1...) while((s32[]{:T(128)}, ...), condition=%wide.region_5.6_spmd.clone, body=%wide.region_2.5_spmd.clone.sunk | while | flops 34611072 | bytes 2157681 | solution.py:187
  346.6 63.8 %all-gather.25.cloned.1.call-done = bf16[1088,4352]{0,1:T(8,128)(2,1)} async-done(((bf16[1088,1088]{0,1:T(8,128)(2,1)}), bf16[1088,4352]{0,1:T(8,128)(2,1)}) %all-gather.25.cloned.1.call-update) | async-done | bytes 9469968 | tf_op jit(solution)/shard_map/all_gather | solution.py:80
  410.4 7.3 convolution_add_fusion
  417.6 91.1 %all-gather.27.cloned.1.call-done = bf16[4352,1088]{0,1:T(8,128)(2,1)} async-done(((bf16[4352,272]{0,1:T(8,128)(2,1)}), bf16[4352,1088]{0,1:T(8,128)(2,1)}) %all-gather.27.cloned.1.call-update) | async-done | bytes 9469968 | tf_op jit(solution)/shard_map/all_gather | solution.py:81
  508.8 7.5 fusion.87
  523.8 133.4 %while.29 = (s32[]{:T(128)}, f32[17,128,64]{1,2,0:T(8,128)}, f32[17,1024,64]{1,2,0:T(8,128)}, f32[17,1024,64]{1,2,0:T(8,128)}, bf16[17,128,64]{2,1,0:T(8,128)(2,...) while((s32[]{:T(128)}, f32[17,128,64]{1,2,0:T(8,128)}, ...), condition=%wide.region_12.13_spmd.clone, body=%wide.region_10.12_spmd.clone.sunk | while | flops 85098368 | bytes 3944593 | solution.py:244
  662.7 9.6 fusion.68
  674.2 35.6 %reduce-scatter.20.cloned.1.call-done = f32[128,1088]{0,1:T(8,128)} async-done(((f32[1024,1088]{0,1:T(8,128)}), f32[128,1088]{0,1:T(8,128)}) %reduce-scatter.20.cloned.1.call-update) | async-done | bytes 557072 | tf_op jit(solution)/shard_map/reduce_scatter | solution.py:250
  711.6 51.4 %reduce-scatter.22.cloned.1.call-done = f32[128,1088]{0,1:T(8,128)} async-done(((f32[1024,1088]{0,1:T(8,128)}), f32[128,1088]{0,1:T(8,128)}) %reduce-scatter.22.cloned.1.call-update) | async-done | bytes 557072 | tf_op jit(solution)/shard_map/reduce_scatter | solution.py:251
  765.8 8.5 fusion.65
  774.9 9.5 fusion.59
  784.5 37.1 %reduce-scatter.36.cloned.1.call-done = f32[136,1088]{1,0:T(8,128)} async-done(((f32[1088,1088]{1,0:T(8,128)}), f32[136,1088]{1,0:T(8,128)}) %reduce-scatter.36.cloned.1.call-update) | async-done | bytes 591888
  824.1 197.3 %reduce-scatter.28.cloned.1.call-done = f32[544,1088]{1,0:T(8,128)} async-done(((f32[4352,1088]{1,0:T(8,128)}), f32[544,1088]{1,0:T(8,128)}) %reduce-scatter.28.cloned.1.call-update) | async-done | bytes 2367504 | tf_op jit(solution)/shard_map/reduce_scatter | solution.py:91
  1021.5 147.7 %reduce-scatter.24.cloned.1.call-done = f32[136,3264]{1,0:T(8,128)} async-done(((f32[1088,3264]{1,0:T(8,128)}), f32[136,3264]{1,0:T(8,128)}) %reduce-scatter.24.cloned.1.call-update) | async-done | bytes 1775632 | tf_op jit(solution)/shard_map/reduce_scatter | solution.py:88
  1172.7 186.2 %reduce-scatter.26.cloned.1.call-done = f32[136,4352]{1,0:T(8,128)} async-done(((f32[1088,4352]{1,0:T(8,128)}), f32[136,4352]{1,0:T(8,128)}) %reduce-scatter.26.cloned.1.call-update) | async-done | bytes 2367504 | tf_op jit(solution)/shard_map/reduce_scatter | solution.py:90
  1386.5 7.3 fusion.49
  1394.0 7.2 multiply_reduce_fusion.1
  1402.6 28.0 %all-reduce.2 = f32[1088,12]{0,1:T(8,128)} all-reduce(f32[1088,12]{0,1:T(8,128)} %concatenate.8), channel_id=12, replica_groups=mesh['dp'=4,'ctx'=8] {'ctx'}, use_global_device_ids=true, to_apply=%region_34.35.clone | all-reduce | flops 13056 | bytes 104448
  1432.0 17.5 %all-reduce.3 = f32[136,12]{0,1:T(8,128)} all-reduce(f32[136,12]{0,1:T(8,128)} %constant_dynamic-slice_fusion.2), channel_id=13, replica_groups=mesh['dp'=4,'ctx'=8] {'dp'}, use_global_device_ids=true, to_apply=%region_35.36.clone | all-reduce | flops 1632 | bytes 13056
  1457.1 11.4 all-reduce.6.cloned.1.call-done
  1479.5 37.7 %reduce-scatter.30.cloned.1.call-done = f32[816,136]{1,0:T(8,128)} async-done(((f32[3264,136]{1,0:T(8,128)}), f32[816,136]{1,0:T(8,128)}) %reduce-scatter.30.cloned.1.call-update) | async-done | bytes 443920
  1521.3 53.7 %reduce-scatter.34.cloned.1.call-done = f32[1088,136]{1,0:T(8,128)} async-done(((f32[4352,136]{1,0:T(8,128)}), f32[1088,136]{1,0:T(8,128)}) %reduce-scatter.34.cloned.1.call-update) | async-done | bytes 591888
  (477 shorter events, 324.4 us)
Async XLA Ops:
  7.2 33.7 %all-gather.13.cloned.1.call-start = ((), (), s32[]{:S(2)}) async-start(), calls=%async_computation.9 | async-start | bytes 2193408 | tf_op jit(solution)/shard_map/all_gather | solution.py:71
  9.0 116.0 %all-gather.15.cloned.1.call-start = ((), (), s32[]{:S(2)}) async-start(), calls=%async_computation.10 | async-start | bytes 9400320 | tf_op jit(solution)/shard_map/all_gather | solution.py:78
  44.9 121.1 %all-gather.23.cloned.1.call-start = ((), (), s32[]{:S(2)}) async-start(), calls=%async_computation.14 | async-start | bytes 2820096 | tf_op jit(solution)/shard_map/all_gather | solution.py:73
  45.7 156.2 %all-gather.29.cloned.1.call-start = ((), (), s32[]{:S(2)}) async-start(), calls=%async_computation.22 | async-start | bytes 3133440 | tf_op jit(solution)/shard_map/all_gather | solution.py:74
  46.9 187.8 %all-gather.17.cloned.1.call-start = ((), (), s32[]{:S(2)}) async-start(), calls=%async_computation.11 | async-start | bytes 2506752 | tf_op jit(solution)/shard_map/all_gather | solution.py:105
  69.4 61.0 %copy-start.32 = (f32[1088]{0:T(1024)}, f32[1088]{0:T(1024)S(1)}, u32[]{:S(2)}) copy-start(f32[1088]{0:T(1024)S(1)} %get-tuple-element.323) | copy-start | bytes 13060
  69.4 61.0 %copy-start.34 = (f32[1088]{0:T(1024)}, f32[1088]{0:T(1024)S(1)}, u32[]{:S(2)}) copy-start(f32[1088]{0:T(1024)S(1)} %get-tuple-element.322) | copy-start | bytes 13060
  69.5 61.0 %copy-start.47 = (f32[128]{0:T(128)}, f32[128]{0:T(128)S(1)}, u32[]{:S(2)}) copy-start(f32[128]{0:T(128)S(1)} %broadcast_multiply_fusion.6) | copy-start | bytes 1540
  69.6 60.8 %copy-start.51 = (f32[128]{0:T(128)}, f32[128]{0:T(128)S(1)}, u32[]{:S(2)}) copy-start(f32[128]{0:T(128)S(1)} %add_rsqrt_fusion.1) | copy-start | bytes 1540
  131.2 136.1 %all-gather.19.cloned.1.call-start = ((), (), s32[]{:S(2)}) async-start(), calls=%async_computation.12 | async-start | bytes 2506752 | tf_op jit(solution)/shard_map/all_gather | solution.py:106
  132.5 210.1 %all-gather.21.cloned.1.call-start = ((), (), s32[]{:S(2)}) async-start(), calls=%async_computation.13 | async-start | bytes 3133440 | tf_op jit(solution)/shard_map/all_gather | solution.py:79
  155.0 255.4 %all-gather.25.cloned.1.call-start = ((), (), s32[]{:S(2)}) async-start(), calls=%async_computation.15 | async-start | bytes 12533760 | tf_op jit(solution)/shard_map/all_gather | solution.py:80
  171.2 337.6 %all-gather.27.cloned.1.call-start = ((), (), s32[]{:S(2)}) async-start(), calls=%async_computation.16 | async-start | bytes 11837440 | tf_op jit(solution)/shard_map/all_gather | solution.py:81
  207.4 502.4 %reduce-scatter.20.cloned.1.call-start = ((), (), s32[]{:S(2)}) async-start(), calls=%async_computation.17 | async-start | bytes 5013504 | tf_op jit(solution)/shard_map/reduce_scatter | solution.py:250
  272.6 70.7 %copy-start.37 = (f32[1088]{0:T(1024)S(1)}, f32[1088]{0:T(1024)}, u32[]{:S(2)}) copy-start(f32[1088]{0:T(1024)} %get-tuple-element.319) | copy-start | bytes 13060
  345.9 64.5 %copy-start.38 = (f32[128]{0:T(128)}, f32[128]{0:T(128)S(1)}, u32[]{:S(2)}) copy-start(f32[128]{0:T(128)S(1)} %broadcast_multiply_fusion.5) | copy-start | bytes 1540
  417.6 98.6 %copy-start.3 = (f32[128,4352]{1,0:T(8,128)}, f32[128,4352]{1,0:T(8,128)S(1)}, u32[]{:S(2)}) copy-start(f32[128,4352]{1,0:T(8,128)S(1)} %convolution_add_fusion) | copy-start | bytes 6684676
  522.2 135.8 %copy-start.5 = (f32[128,1088]{0,1:T(8,128)}, f32[128,1088]{0,1:T(8,128)S(1)}, u32[]{:S(2)}) copy-start(f32[128,1088]{0,1:T(8,128)S(1)} %get-tuple-element.382) | copy-start | bytes 1671172
  657.3 105.8 %reduce-scatter.22.cloned.1.call-start = ((), (), s32[]{:S(2)}) async-start(), calls=%async_computation.18 | async-start | bytes 5013504 | tf_op jit(solution)/shard_map/reduce_scatter | solution.py:251
  658.0 163.6 %reduce-scatter.36.cloned.1.call-start = ((), (), s32[]{:S(2)}) async-start(), calls=%async_computation.27 | async-start | bytes 5640192
  661.1 360.4 %reduce-scatter.28.cloned.1.call-start = ((), (), s32[]{:S(2)}) async-start(), calls=%async_computation.21 | async-start | bytes 22560768 | tf_op jit(solution)/shard_map/reduce_scatter | solution.py:91
  672.3 93.5 %copy-start.48 = (f32[128]{0:T(128)S(1)}, f32[128]{0:T(128)}, u32[]{:S(2)}) copy-start(f32[128]{0:T(128)} %copy-done.47) | copy-start | bytes 1540
  672.3 496.9 %reduce-scatter.24.cloned.1.call-start = ((), (), s32[]{:S(2)}) async-start(), calls=%async_computation.19 | async-start | bytes 16293888 | tf_op jit(solution)/shard_map/reduce_scatter | solution.py:88
  774.3 584.6 %reduce-scatter.26.cloned.1.call-start = ((), (), s32[]{:S(2)}) async-start(), calls=%async_computation.20 | async-start | bytes 21307392 | tf_op jit(solution)/shard_map/reduce_scatter | solution.py:90
  784.5 669.4 %reduce-scatter.32.cloned.1.call-start = ((), (), s32[]{:S(2)}) async-start(), calls=%async_computation.24 | async-start | bytes 1392640
  824.1 644.4 %all-reduce.6.cloned.1.call-start = ((), (), s32[]{:S(2)}) async-start(), calls=%async_computation.26 | async-start | bytes 5013504
  1021.5 495.7 %reduce-scatter.30.cloned.1.call-start = ((), (), s32[]{:S(2)}) async-start(), calls=%async_computation.23 | async-start | bytes 4177920
  1172.7 402.3 %reduce-scatter.34.cloned.1.call-start = ((), (), s32[]{:S(2)}) async-start(), calls=%async_computation.25 | async-start | bytes 5570560
  1394.0 58.2 %copy-start.6 = (f32[128,1088]{0,1:T(8,128)S(1)}, f32[128,1088]{0,1:T(8,128)}, u32[]{:S(2)}) copy-start(f32[128,1088]{0,1:T(8,128)} %copy-done.5) | copy-start | bytes 1671172
  1402.6 66.0 %copy-start.9 = (f32[544,272]{1,0:T(8,128)S(1)}, f32[544,272]{1,0:T(8,128)}, u32[]{:S(2)}) copy-start(f32[544,272]{1,0:T(8,128)} %copy.103) | copy-start | bytes 1775620
  1402.6 66.0 %copy-start.10 = (f32[544,272]{1,0:T(8,128)S(1)}, f32[544,272]{1,0:T(8,128)}, u32[]{:S(2)}) copy-start(f32[544,272]{1,0:T(8,128)} %copy.100) | copy-start | bytes 1775620
  1518.6 58.0 %copy-start.30 = (f32[136,1088]{1,0:T(8,128)S(1)}, f32[136,1088]{1,0:T(8,128)}, u32[]{:S(2)}) copy-start(f32[136,1088]{1,0:T(8,128)} %param.32) | copy-start | bytes 1775620
  (44 other events, 428.4 us)
Sparse Core Ops, SparseCore 0:
  10.2 30.6 all-gather.12
  45.0 79.9 all-gather.14
  127.2 38.7 all-gather.22
  168.1 33.8 all-gather.28
  203.9 30.6 all-gather.16
  236.7 30.5 all-gather.18
  269.7 37.5 all-gather.20
  309.2 101.1 all-gather.24
  412.2 96.4 all-gather.26
  657.4 52.3 reduce-scatter.19
  712.1 50.8 reduce-scatter.21
  765.2 56.3 reduce-scatter.35
  824.0 197.4 reduce-scatter.27
  1023.6 145.5 reduce-scatter.23
  1171.4 187.4 reduce-scatter.25
  1361.7 26.8 reduce-scatter.31
  1391.6 76.8 all-reduce.5
  1471.4 45.6 reduce-scatter.29
  1520.2 54.7 reduce-scatter.33
where the time goes:
time: 1600 us; the launch traced here: 1590 us
  waiting for transfers between devices  1090 us (68%)
  matrix products  234 us (15%)
  local copies, waits for them, and re-layouts  113 us (7%)
  blocking collectives  88.3 us (6%)
  other arithmetic  38.1 us (2%)
  between operations  16.8 us (1%)
    reduce_scatter x1, waiting for transfers between devices, reduce_grads(): lax.psum_scatter(fourth_part, 'ctx', scatter_dimension=0, tiled=True)  197 us
    reduce_scatter x1, waiting for transfers between devices, reduce_grads(): lax.psum_scatter(third_part, 'ctx', scatter_dimension=0, tiled=True)  186 us
    reduce_scatter x1, waiting for transfers between devices, reduce_grads(): lax.psum_scatter(first_part, 'ctx', scatter_dimension=0, tiled=True)  148 us
    unnamed x24, waiting for transfers between devices  141 us
    all_gather x1, waiting for transfers between devices, gather_params(): lax.all_gather(piece_four, 'dp', axis=1, tiled=True)  91.1 us
    all_gather x1, waiting for transfers between devices, gather_params(): lax.all_gather(piece_three, 'dp', axis=1, tiled=True)  63.8 us
    all_gather x1, waiting for transfers between devices, gather_params(): lax.all_gather(piece_one, 'dp', axis=1, tiled=True)  55.4 us
    reduce_scatter x1, waiting for transfers between devices, local(): lax.psum_scatter(join_heads(dvalue_heads), 'ctx', scatter_dimension=0, ti...  51.4 us
  transfers between devices with their start and end apart: 19, of which 17 were waited for; matrix products, arithmetic and copies ran while one was open for 14% of the time, Pallas kernels for 0%

commit v1 on v0

--- a/solution.py
+++ b/solution.py
@@ -1,7 +1,9 @@
+import functools
 import jax
 import jax.numpy as jnp
 from jax import lax
 from jax.sharding import PartitionSpec as P
+from jax.lax import axis_index, ppermute, psum
 
 D = 1088
 H = 17
@@ -18,6 +20,22 @@
 masked_score = -1e30
 
 
+def close_block(work_x, mesh_dim):
+    slots = psum(1, mesh_dim)
+    row_list = [work_x]
+    for w in range(1, slots):
+        row_list.append(
+            ppermute(
+                row_list[w - 1], mesh_dim, perm=[(ix, (ix - 1) % slots) for ix in range(slots)]
+            )
+        )
+    piece_now = jnp.concatenate(row_list, axis=1)
+    return jnp.roll(piece_now, shift=axis_index(mesh_dim) * work_x.shape[1], axis=1)
+
+
+_bind_points = functools.partial(close_block, mesh_dim="dp")
+
+
 def layer_norm(values):
     center = jnp.mean(values, axis=-1, keepdims=True)
     shifted = values - center
@@ -78,7 +96,7 @@
         lax.all_gather(piece_one, "dp", axis=1, tiled=True),
         lax.all_gather(piece_two, "dp", axis=1, tiled=True),
         lax.all_gather(piece_three, "dp", axis=1, tiled=True),
-        lax.all_gather(piece_four, "dp", axis=1, tiled=True),
+        _bind_points(piece_four),
         lax.all_gather(piece_five, "dp", axis=1, tiled=True),
     )
 

time: 1600 us -> 1540 us (0.963)
  waiting for transfers between devices: 1090 us -> 1040 us
  local copies, waits for them, and re-layouts: 113 us -> 75.8 us
  other arithmetic: 38.1 us -> 73.7 us
    ppermute x0 -> x3, waiting for transfers between devices: none -> 132 us  [close_block(): ppermute(row_list[w - 1], mesh_dim, perm=[(ix, (ix - 1) % slots) for ix i...]
    all_gather x1 -> x0, waiting for transfers between devices: 91.1 us -> none  [gather_params(): lax.all_gather(piece_four, 'dp', axis=1, tiled=True)]
    all_gather x1, waiting for transfers between devices: 63.8 us -> 23.7 us  [gather_params(): lax.all_gather(piece_three, 'dp', axis=1, tiled=True)]
    concatenate x0 -> x1, other arithmetic: none -> 37.9 us  [close_block(): jnp.roll(piece_now, shift=axis_index(mesh_dim) * work_x.shape[1], axis=1)]
    all_gather x1, waiting for transfers between devices: 27.4 us -> 0.01 us  [gather_keys(): lax.all_gather(value_rows, 'ctx', axis=0, tiled=True)]
    all_gather x1, waiting for transfers between devices: 26 us -> 0.02 us  [gather_keys(): lax.all_gather(key_rows, 'ctx', axis=0, tiled=True)]
    dynamic_update_slice x17, local copies, waits for them, and re-layouts: 22.1 us -> 0.63 us  [local(): lax.map(head_forward, (heads_query, heads_key, heads_value))]
    unnamed x132 -> x118, local copies, waits for them, and re-layouts: 41 us -> 38.2 us
  transfers between devices with their start and end apart: 19 -> 21, of which waited for: 17 -> 16; matrix products, arithmetic and copies ran while one was open for 14% -> 15% of each run, Pallas kernels for 0% -> 0%
where the time goes in v1:
time: 1540 us; the launch traced here: 1530 us
  waiting for transfers between devices  1040 us (68%)
  matrix products  233 us (15%)
  blocking collectives  83 us (5%)
  local copies, waits for them, and re-layouts  75.8 us (5%)
  other arithmetic  73.7 us (5%)
  between operations  17 us (1%)
    reduce_scatter x1, waiting for transfers between devices, reduce_grads(): lax.psum_scatter(fourth_part, 'ctx', scatter_dimension=0, tiled=True)  197 us
    reduce_scatter x1, waiting for transfers between devices, reduce_grads(): lax.psum_scatter(third_part, 'ctx', scatter_dimension=0, tiled=True)  186 us
    reduce_scatter x1, waiting for transfers between devices, reduce_grads(): lax.psum_scatter(first_part, 'ctx', scatter_dimension=0, tiled=True)  148 us
    unnamed x23, waiting for transfers between devices  144 us
    ppermute x3, waiting for transfers between devices, close_block(): ppermute(row_list[w - 1], mesh_dim, perm=[(ix, (ix - 1) % slots) for ix i...  132 us
    all_gather x1, waiting for transfers between devices, gather_params(): lax.all_gather(piece_one, 'dp', axis=1, tiled=True)  55.4 us
    reduce_scatter x1, waiting for transfers between devices, local(): lax.psum_scatter(join_heads(dvalue_heads), 'ctx', scatter_dimension=0, ti...  51.3 us
    unnamed x2, blocking collectives  45.7 us
  transfers between devices with their start and end apart: 21, of which 16 were waited for; matrix products, arithmetic and copies ran while one was open for 15% of the time, Pallas kernels for 0%

profile of v1, /device:TPU:0, one launch (start us, length us, event | category | flops | bytes accessed | tf_op | source)
XLA Modules:
  0.0 1529.6 jit_solution(17099568616590615897)
XLA Ops:
  9.1 31.8 %all-gather.12.cloned.1.call-done = bf16[1088,816]{1,0:T(8,128)(2,1)} async-done(((bf16[136,816]{1,0:T(8,128)(2,1)}), bf16[1088,816]{1,0:T(8,128)(2,1)}) %all-gather.12.cloned.1.call-update) | async-done | bytes 1775632 | tf_op jit(solution)/shard_map/all_gather | solution.py:89
  46.9 12.8 all-gather
  59.8 8.8 all-gather.1
  69.6 55.4 %all-gather.14.cloned.1.call-done = bf16[1088,3264]{0,1:T(8,128)(2,1)} async-done(((bf16[1088,816]{0,1:T(8,128)(2,1)}), bf16[1088,3264]{0,1:T(8,128)(2,1)}) %all-gather.14.cloned.1.call-update) | async-done | bytes 7102480 | tf_op jit(solution)/shard_map/all_gather | solution.py:96
  125.0 5.4 fusion.83
  132.5 29.9 %all-gather.26.cloned.1.call-done = bf16[8,544,272]{1,2,0:T(8,128)(2,1)} async-done(((bf16[1,544,272]{1,2,0:T(8,128)(2,1)}), bf16[8,544,272]{1,2,0:T(8,128)(2,1)}) %all-gather.26.cloned.1.call-update) | async-done | bytes 2367504 | tf_op jit(solution)/shard_map/all_gather | solution.py:92
  170.2 51.5 %collective-permute-done = bf16[4352,272]{0,1:T(8,128)(2,1)} collective-permute-done((bf16[4352,272]{0,1:T(8,128)(2,1)}, bf16[4352,272]{0,1:T(8,128)(2,1)}, u32[]{:S(2)}, u32[]{:S(2)}) %collective-permute-start) | collective-permute-done | bytes 2367520 | tf_op jit(solution)/shard_map/ppermute | solution.py:28
  225.0 15.8 %all_gather.48 = bf16[1088,272]{1,0:T(8,128)(2,1)S(1)} all-gather(bf16[136,272]{1,0:T(8,128)(2,1)S(1)} %convert_element_type.74), channel_id=1, replica_groups=mesh['dp'=4,'ctx'=8] {'ctx'}, dimensions={0}, use_global_device_ids=true | all-gather | bytes 665856 | tf_op jit(solution)/shard_map/all_gather | solution.py:90
  242.0 38.5 %collective-permute-done.1 = bf16[4352,272]{0,1:T(8,128)(2,1)} collective-permute-done((bf16[4352,272]{0,1:T(8,128)(2,1)}, bf16[4352,272]{0,1:T(8,128)(2,1)}, u32[]{:S(2)}, u32[]{:S(2)}) %collective-permute-start.1) | collective-permute-done | bytes 2367520 | tf_op jit(solution)/shard_map/ppermute | solution.py:28
  290.5 42.5 %collective-permute-done.2 = bf16[4352,272]{0,1:T(8,128)(2,1)} collective-permute-done((bf16[4352,272]{0,1:T(8,128)(2,1)}, bf16[4352,272]{0,1:T(8,128)(2,1)}, u32[]{:S(2)}, u32[]{:S(2)}) %collective-permute-start.2) | collective-permute-done | bytes 2367520 | tf_op jit(solution)/shard_map/ppermute | solution.py:28
  333.0 37.9 %fusion.50 = bf16[4352,1088]{0,1:T(8,128)(2,1)} fusion(s32[]{:T(128)S(6)} %select_n.24, bf16[4352,272]{0,1:T(8,128)(2,1)S(1)} %copy-done.4, bf16[4352,272]{0,1:T(8,128)(2,1)} %collective-permute-done, bf16[4352,272]{0,1:T(8,128)(2,1)} %collective-permute-done.1, bf16[4352,272]{0,1:T(8,128)(2,1)} %collective-permute-done.2), kind=kLoop, calls=%fused_computation.69 | loop fusion | flops 75759616 | bytes 18939908 | tf_op jit(solution)/shard_map/jit(_roll_dynamic)/concatenate | solution.py:33
  381.7 48.4 %while.28 = (s32[]{:T(128)}, bf16[17,128,64]{1,2,0:T(8,128)(2,1)S(1)}, f32[17,128]{1,0:T(8,128)S(1)}, bf16[17,128,64]{2,1,0:T(8,128)(2,1)S(1)}, bf16[17,1024,64]...) while((s32[]{:T(128)}, ...), condition=%wide.region_5.6_spmd.clone, body=%wide.region_2.5_spmd.clone.sunk | while | flops 34611072 | bytes 2157681 | solution.py:205
  433.7 23.7 %all-gather.24.cloned.1.call-done = bf16[1088,4352]{0,1:T(8,128)(2,1)} async-done(((bf16[1088,1088]{0,1:T(8,128)(2,1)}), bf16[1088,4352]{0,1:T(8,128)(2,1)}) %all-gather.24.cloned.1.call-update) | async-done | bytes 9469968 | tf_op jit(solution)/shard_map/all_gather | solution.py:98
  457.4 7.3 convolution_add_fusion
  464.8 7.5 fusion.95
  478.5 122.2 %while.29 = (s32[]{:T(128)}, f32[17,128,64]{1,2,0:T(8,128)}, f32[17,1024,64]{1,2,0:T(8,128)}, f32[17,1024,64]{1,2,0:T(8,128)}, bf16[17,128,64]{2,1,0:T(8,128)(2,...) while((s32[]{:T(128)}, f32[17,128,64]{1,2,0:T(8,128)}, ...), condition=%wide.region_12.14_spmd.clone, body=%wide.region_10.13_spmd.clone.sunk | while | flops 85098368 | bytes 3944593 | solution.py:262
  606.1 9.7 fusion.76
  617.7 35.7 %reduce-scatter.20.cloned.1.call-done = f32[128,1088]{0,1:T(8,128)} async-done(((f32[1024,1088]{0,1:T(8,128)}), f32[128,1088]{0,1:T(8,128)}) %reduce-scatter.20.cloned.1.call-update) | async-done | bytes 557072 | tf_op jit(solution)/shard_map/reduce_scatter | solution.py:268
  655.1 51.3 %reduce-scatter.22.cloned.1.call-done = f32[128,1088]{0,1:T(8,128)} async-done(((f32[1024,1088]{0,1:T(8,128)}), f32[128,1088]{0,1:T(8,128)}) %reduce-scatter.22.cloned.1.call-update) | async-done | bytes 557072 | tf_op jit(solution)/shard_map/reduce_scatter | solution.py:269
  709.2 8.4 fusion.73
  717.7 9.6 fusion.67
  727.3 37.8 %reduce-scatter.36.cloned.1.call-done = f32[136,1088]{1,0:T(8,128)} async-done(((f32[1088,1088]{1,0:T(8,128)}), f32[136,1088]{1,0:T(8,128)}) %reduce-scatter.36.cloned.1.call-update) | async-done | bytes 591888
  767.6 197.2 %reduce-scatter.28.cloned.1.call-done = f32[544,1088]{1,0:T(8,128)} async-done(((f32[4352,1088]{1,0:T(8,128)}), f32[544,1088]{1,0:T(8,128)}) %reduce-scatter.28.cloned.1.call-update) | async-done | bytes 2367504 | tf_op jit(solution)/shard_map/reduce_scatter | solution.py:109
  964.9 147.8 %reduce-scatter.24.cloned.1.call-done = f32[136,3264]{1,0:T(8,128)} async-done(((f32[1088,3264]{1,0:T(8,128)}), f32[136,3264]{1,0:T(8,128)}) %reduce-scatter.24.cloned.1.call-update) | async-done | bytes 1775632 | tf_op jit(solution)/shard_map/reduce_scatter | solution.py:106
  1116.2 186.2 %reduce-scatter.26.cloned.1.call-done = f32[136,4352]{1,0:T(8,128)} async-done(((f32[1088,4352]{1,0:T(8,128)}), f32[136,4352]{1,0:T(8,128)}) %reduce-scatter.26.cloned.1.call-update) | async-done | bytes 2367504 | tf_op jit(solution)/shard_map/reduce_scatter | solution.py:108
  1323.9 7.4 fusion.57
  1331.4 7.1 multiply_reduce_fusion.1
  1343.2 27.9 %all-reduce.2 = f32[1088,12]{0,1:T(8,128)} all-reduce(f32[1088,12]{0,1:T(8,128)} %concatenate.16), channel_id=12, replica_groups=mesh['dp'=4,'ctx'=8] {'ctx'}, use_global_device_ids=true, to_apply=%region_34.36.clone | all-reduce | flops 13056 | bytes 104448
  1372.5 17.8 %all-reduce.3 = f32[136,12]{0,1:T(8,128)} all-reduce(f32[136,12]{0,1:T(8,128)} %constant_dynamic-slice_fusion.2), channel_id=13, replica_groups=mesh['dp'=4,'ctx'=8] {'dp'}, use_global_device_ids=true, to_apply=%region_35.37.clone | all-reduce | flops 1632 | bytes 13056
  1398.0 13.9 all-reduce.6.cloned.1.call-done
  1422.8 37.7 %reduce-scatter.30.cloned.1.call-done = f32[816,136]{1,0:T(8,128)} async-done(((f32[3264,136]{1,0:T(8,128)}), f32[816,136]{1,0:T(8,128)}) %reduce-scatter.30.cloned.1.call-update) | async-done | bytes 443920
  1464.6 53.6 %reduce-scatter.34.cloned.1.call-done = f32[1088,136]{1,0:T(8,128)} async-done(((f32[4352,136]{1,0:T(8,128)}), f32[1088,136]{1,0:T(8,128)}) %reduce-scatter.34.cloned.1.call-update) | async-done | bytes 591888
  (468 shorter events, 293.4 us)
Async XLA Ops:
  7.2 33.7 %all-gather.12.cloned.1.call-start = ((), (), s32[]{:S(2)}) async-start(), calls=%async_computation.9 | async-start | bytes 2193408 | tf_op jit(solution)/shard_map/all_gather | solution.py:89
  9.0 116.0 %all-gather.14.cloned.1.call-start = ((), (), s32[]{:S(2)}) async-start(), calls=%async_computation.10 | async-start | bytes 9400320 | tf_op jit(solution)/shard_map/all_gather | solution.py:96
  44.9 117.5 %all-gather.26.cloned.1.call-start = ((), (), s32[]{:S(2)}) async-start(), calls=%async_computation.21 | async-start | bytes 3133440 | tf_op jit(solution)/shard_map/all_gather | solution.py:92
  45.8 239.3 %all-gather.22.cloned.1.call-start = ((), (), s32[]{:S(2)}) async-start(), calls=%async_computation.14 | async-start | bytes 2820096 | tf_op jit(solution)/shard_map/all_gather | solution.py:91
  46.8 324.4 %all-gather.16.cloned.1.call-start = ((), (), s32[]{:S(2)}) async-start(), calls=%async_computation.11 | async-start | bytes 2506752 | tf_op jit(solution)/shard_map/all_gather | solution.py:123
  69.4 61.0 %copy-start.30 = (f32[1088]{0:T(1024)}, f32[1088]{0:T(1024)S(1)}, u32[]{:S(2)}) copy-start(f32[1088]{0:T(1024)S(1)} %get-tuple-element.324) | copy-start | bytes 13060
  69.4 61.0 %copy-start.35 = (f32[1088]{0:T(1024)}, f32[1088]{0:T(1024)S(1)}, u32[]{:S(2)}) copy-start(f32[1088]{0:T(1024)S(1)} %get-tuple-element.323) | copy-start | bytes 13060
  131.2 245.2 %all-gather.18.cloned.1.call-start = ((), (), s32[]{:S(2)}) async-start(), calls=%async_computation.12 | async-start | bytes 2506752 | tf_op jit(solution)/shard_map/all_gather | solution.py:124
  132.5 297.7 %all-gather.20.cloned.1.call-start = ((), (), s32[]{:S(2)}) async-start(), calls=%async_computation.13 | async-start | bytes 3133440 | tf_op jit(solution)/shard_map/all_gather | solution.py:97
  167.8 116.0 %copy-start.44 = (s32[8,2]{0,1:T(2,128)S(1)}, s32[8,2]{0,1:T(2,128)}, u32[]{:S(2)}) copy-start(s32[8,2]{0,1:T(2,128)} %param.26) | copy-start | bytes 196
  167.8 53.9 %collective-permute-start = (bf16[4352,272]{0,1:T(8,128)(2,1)}, bf16[4352,272]{0,1:T(8,128)(2,1)}, u32[]{:S(2)}, u32[]{:S(2)}) collective-permute-start(bf16[4352,272]{0,1:T(8,128)(2,1)} %reshape.198), channel_id=1, source_target_pairs={{0,24},{8,0},{16,8},{24,16},{1,25},{9,1},{17,9},{25,17},{2,26},{10... | collective-permute-start | bytes 7102472 | tf_op jit(solution)/shard_map/ppermute | solution.py:28
  221.7 58.7 %collective-permute-start.1 = (bf16[4352,272]{0,1:T(8,128)(2,1)}, bf16[4352,272]{0,1:T(8,128)(2,1)}, u32[]{:S(2)}, u32[]{:S(2)}) collective-permute-start(bf16[4352,272]{0,1:T(8,128)(2,1)} %collective-permute-done), channel_id=1, source_target_pairs={{0,24},{8,0},{16,8},{24,16},{1,25},{9,1},{17,9},{25,17},{2,26},{10... | collective-permute-start | bytes 7102472 | tf_op jit(solution)/shard_map/ppermute | solution.py:28
  242.0 215.5 %all-gather.24.cloned.1.call-start = ((), (), s32[]{:S(2)}) async-start(), calls=%async_computation.15 | async-start | bytes 12533760 | tf_op jit(solution)/shard_map/all_gather | solution.py:98
  280.5 52.5 %collective-permute-start.2 = (bf16[4352,272]{0,1:T(8,128)(2,1)}, bf16[4352,272]{0,1:T(8,128)(2,1)}, u32[]{:S(2)}, u32[]{:S(2)}) collective-permute-start(bf16[4352,272]{0,1:T(8,128)(2,1)} %collective-permute-done.1), channel_id=1, source_target_pairs={{0,24},{8,0},{16,8},{24,16},{1,25},{9,1},{17,9},{25,17},{2,26},{10... | collective-permute-start | bytes 7102472 | tf_op jit(solution)/shard_map/ppermute | solution.py:28
  290.3 80.6 %copy-start.20 = (bf16[128,1088]{0,1:T(8,128)(2,1)S(1)}, bf16[128,1088]{0,1:T(8,128)(2,1)}, u32[]{:S(2)}) copy-start(bf16[128,1088]{0,1:T(8,128)(2,1)} %get-tuple-element.387) | copy-start | bytes 835588
  290.3 363.0 %reduce-scatter.20.cloned.1.call-start = ((), (), s32[]{:S(2)}) async-start(), calls=%async_computation.16 | async-start | bytes 5013504 | tf_op jit(solution)/shard_map/reduce_scatter | solution.py:268
  477.1 124.3 %copy-start.5 = (f32[128,1088]{0,1:T(8,128)}, f32[128,1088]{0,1:T(8,128)S(1)}, u32[]{:S(2)}) copy-start(f32[128,1088]{0,1:T(8,128)S(1)} %get-tuple-element.383) | copy-start | bytes 1671172
  600.8 105.6 %reduce-scatter.22.cloned.1.call-start = ((), (), s32[]{:S(2)}) async-start(), calls=%async_computation.17 | async-start | bytes 5013504 | tf_op jit(solution)/shard_map/reduce_scatter | solution.py:269
  601.3 163.8 %reduce-scatter.36.cloned.1.call-start = ((), (), s32[]{:S(2)}) async-start(), calls=%async_computation.26 | async-start | bytes 5640192
  604.5 360.3 %reduce-scatter.28.cloned.1.call-start = ((), (), s32[]{:S(2)}) async-start(), calls=%async_computation.20 | async-start | bytes 22560768 | tf_op jit(solution)/shard_map/reduce_scatter | solution.py:109
  615.7 93.4 %copy-start.31 = (f32[1088]{0:T(1024)S(1)}, f32[1088]{0:T(1024)}, u32[]{:S(2)}) copy-start(f32[1088]{0:T(1024)} %copy-done.30) | copy-start | bytes 13060
  615.8 93.4 %copy-start.36 = (f32[1088]{0:T(1024)S(1)}, f32[1088]{0:T(1024)}, u32[]{:S(2)}) copy-start(f32[1088]{0:T(1024)} %copy-done.35) | copy-start | bytes 13060
  615.8 93.4 %copy-start.41 = (f32[128]{0:T(128)S(1)}, f32[128]{0:T(128)}, u32[]{:S(2)}) copy-start(f32[128]{0:T(128)} %copy-done.40) | copy-start | bytes 1540
  615.8 496.9 %reduce-scatter.24.cloned.1.call-start = ((), (), s32[]{:S(2)}) async-start(), calls=%async_computation.18 | async-start | bytes 16293888 | tf_op jit(solution)/shard_map/reduce_scatter | solution.py:106
  717.6 584.8 %reduce-scatter.26.cloned.1.call-start = ((), (), s32[]{:S(2)}) async-start(), calls=%async_computation.19 | async-start | bytes 21307392 | tf_op jit(solution)/shard_map/reduce_scatter | solution.py:108
  727.3 667.4 %reduce-scatter.32.cloned.1.call-start = ((), (), s32[]{:S(2)}) async-start(), calls=%async_computation.23 | async-start | bytes 1392640
  767.6 644.2 %all-reduce.6.cloned.1.call-start = ((), (), s32[]{:S(2)}) async-start(), calls=%async_computation.25 | async-start | bytes 5013504
  964.8 495.6 %reduce-scatter.30.cloned.1.call-start = ((), (), s32[]{:S(2)}) async-start(), calls=%async_computation.22 | async-start | bytes 4177920
  1116.1 402.0 %reduce-scatter.34.cloned.1.call-start = ((), (), s32[]{:S(2)}) async-start(), calls=%async_computation.24 | async-start | bytes 5570560
  1331.4 61.6 %copy-start.6 = (f32[128,1088]{0,1:T(8,128)S(1)}, f32[128,1088]{0,1:T(8,128)}, u32[]{:S(2)}) copy-start(f32[128,1088]{0,1:T(8,128)} %copy-done.5) | copy-start | bytes 1671172
  1338.4 73.4 %copy-start.9 = (f32[544,272]{1,0:T(8,128)S(1)}, f32[544,272]{1,0:T(8,128)}, u32[]{:S(2)}) copy-start(f32[544,272]{1,0:T(8,128)} %copy.103) | copy-start | bytes 1775620
  1338.4 73.4 %copy-start.10 = (f32[544,272]{1,0:T(8,128)S(1)}, f32[544,272]{1,0:T(8,128)}, u32[]{:S(2)}) copy-start(f32[544,272]{1,0:T(8,128)} %copy.100) | copy-start | bytes 1775620
  (39 other events, 826.3 us)
Sparse Core Ops, SparseCore 0:
  10.2 30.6 all-gather.11
  45.0 79.9 all-gather.13
  127.2 35.0 all-gather.25
  164.5 31.7 all-gather.21
  198.3 31.4 all-gather.15
  231.8 31.3 all-gather.17
  265.6 88.7 all-gather.19
  356.3 101.1 all-gather.23
  600.9 52.3 reduce-scatter.19
  655.5 50.8 reduce-scatter.21
  708.7 56.3 reduce-scatter.35
  767.3 197.4 reduce-scatter.27
  967.1 145.5 reduce-scatter.23
  1114.9 187.4 reduce-scatter.25
  1305.2 26.8 reduce-scatter.31
  1335.2 76.5 all-reduce.5
  1414.7 45.6 reduce-scatter.29
  1463.3 54.7 reduce-scatter.33
